TPU v7x, 32 devices: a whole 2x2x4 slice. The times are simulated.
32 devices in a mesh: fsdp: 8 (over z, y), ctx: 2 (over x), tp: 2 (over core).
Axes of the slice: x: 2, y: 2, z: 4, core: 2. Of those that a mesh axis runs over, the one named last changes fastest.
Arguments:
- inputs: bfloat16 [2, 16, 592, 1024], P(None, ('fsdp', 'tp'), 'ctx'), may hold values from -6 to 6
- cotangent: bfloat16 [2, 16, 592, 1024], P(None, ('fsdp', 'tp'), 'ctx'), may hold values from -6 to 6
- slot_mask: int32 [2, 16], P(None, ('fsdp', 'tp')), may hold values 0 or 1
- key_mask: int32 [2, 16, 592], P(None, 'fsdp'), may hold values from 0 to 1, as said below
- ln1_gain: bfloat16 [1024], P('fsdp'), may hold values from 0.5 to 1.5
- ln1_bias: bfloat16 [1024], P('fsdp'), may hold values from -0.796875 to 0.796875
- w_qkv: bfloat16 [1024, 3, 1024], P('fsdp', None, 'tp'), may hold values from -0.1875 to 0.1875
- b_qv: bfloat16 [2, 16, 64], P(None, 'tp', 'fsdp'), may hold values from -0.796875 to 0.796875
- w_out: bfloat16 [1024, 1024], P('tp', 'fsdp'), may hold values from -2.5 to 2.5
- b_out: bfloat16 [1024], P('fsdp'), may hold values from -0.796875 to 0.796875
- ln2_gain: bfloat16 [1024], P('fsdp'), may hold values from 0.5 to 1.5
- ln2_bias: bfloat16 [1024], P('fsdp'), may hold values from -0.796875 to 0.796875
- w_fc1: bfloat16 [1024, 4096], P('fsdp', 'tp'), may hold values from -0.1875 to 0.1875
- b_fc1: bfloat16 [64, 64], P('tp', 'fsdp'), may hold values from -0.796875 to 0.796875
- w_fc2: bfloat16 [4096, 1024], P('tp', 'fsdp'), may hold values from -0.09375 to 0.09375
- b_fc2: bfloat16 [1024], P('fsdp'), may hold values from -0.796875 to 0.796875
Outputs:
- outputs: bfloat16 [2, 16, 592, 1024], P(None, ('fsdp', 'tp'), 'ctx')
- input_grad: bfloat16 [2, 16, 592, 1024], P(None, ('fsdp', 'tp'), 'ctx')
- ln1_gain_grad: float32 [1024], P(('fsdp', 'ctx', 'tp'))
- ln1_bias_grad: float32 [1024], P(('fsdp', 'ctx', 'tp'))
- w_qkv_grad: float32 [1024, 3, 1024], P(('fsdp', 'ctx'), None, 'tp')
- b_qv_grad: float32 [2, 16, 64], P(None, 'tp', ('fsdp', 'ctx'))
- w_out_grad: float32 [1024, 1024], P('tp', ('fsdp', 'ctx'))
- b_out_grad: float32 [1024], P(('fsdp', 'ctx', 'tp'))
- ln2_gain_grad: float32 [1024], P(('fsdp', 'ctx', 'tp'))
- ln2_bias_grad: float32 [1024], P(('fsdp', 'ctx', 'tp'))
- w_fc1_grad: float32 [1024, 4096], P(('fsdp', 'ctx'), 'tp')
- b_fc1_grad: float32 [64, 64], P('tp', ('fsdp', 'ctx'))
- w_fc2_grad: float32 [4096, 1024], P('tp', ('fsdp', 'ctx'))
- b_fc2_grad: float32 [1024], P(('fsdp', 'ctx', 'tp'))
Inputs may be any that keep to these rules, and one draw needn't show every extreme that they name: `key_mask`: position 0 of every image is 1; positions 577 and beyond are 0.
All inputs are finite; a program needn't handle non-finite values. No bound on the sum of `slot_mask` on one device may be relied on, other than what follows from the above.
Results may differ from a plain program's by a relative error of at most 0.023.
Values may be sent and summed in bfloat16 or wider, within the bound.
A program may use at most 256 MiB of HBM per device.

v0:
```python
import jax
import jax.numpy as jnp
from jax import lax
from jax.sharding import PartitionSpec as P

HD = 64
SEQ_LEN = 577


def normalize_rows(values, gain_row, shift_row):
    average = jnp.mean(values, axis=-1, keepdims=True)
    centred = values - average
    inv_std = lax.rsqrt(jnp.mean(centred * centred, axis=-1, keepdims=True) + 1e-05)
    normed = centred * inv_std
    return (normed, inv_std, normed * gain_row + shift_row)


def normalize_back(upstream, normed, inv_std, gain_row):
    scaled = upstream * gain_row
    inner_term = (
        scaled
        - jnp.mean(scaled, axis=-1, keepdims=True)
        - normed * jnp.mean(scaled * normed, axis=-1, keepdims=True)
    )
    return inv_std * inner_term


def masked_scores(query_heads, key_heads, valid_keys):
    scores = (
        jnp.einsum("gqhd,gkhd->ghqk", query_heads, key_heads, preferred_element_type=jnp.float32)
        * 0.125
    )
    return jnp.where(valid_keys[:, None, None, :], scores, -jnp.inf)


def row_product(source, weight, einsum_form):
    return jnp.einsum(einsum_form, source, weight, preferred_element_type=jnp.float32)


def body(
    inputs,
    cotangent,
    slot_mask,
    key_mask,
    ln1_gain,
    ln1_bias,
    w_qkv,
    b_qv,
    w_out,
    b_out,
    ln2_gain,
    ln2_bias,
    w_fc1,
    b_fc1,
    w_fc2,
    b_fc2,
):
    gathered = (
        lax.all_gather(ln1_gain, "fsdp", axis=0, tiled=True),
        lax.all_gather(ln1_bias, "fsdp", axis=0, tiled=True),
        lax.all_gather(ln2_gain, "fsdp", axis=0, tiled=True),
        lax.all_gather(ln2_bias, "fsdp", axis=0, tiled=True),
        lax.all_gather(b_out, "fsdp", axis=0, tiled=True),
        lax.all_gather(b_fc2, "fsdp", axis=0, tiled=True),
        lax.all_gather(w_qkv, "fsdp", axis=0, tiled=True),
        lax.all_gather(b_qv, "fsdp", axis=2, tiled=True),
        lax.all_gather(w_out, "fsdp", axis=1, tiled=True),
        lax.all_gather(w_fc1, "fsdp", axis=0, tiled=True),
        lax.all_gather(b_fc1, "fsdp", axis=1, tiled=True),
        lax.all_gather(w_fc2, "fsdp", axis=1, tiled=True),
    )
    gain_one = gathered[0].astype(jnp.float32)
    shift_one = gathered[1].astype(jnp.float32)
    gain_two = gathered[2].astype(jnp.float32)
    shift_two = gathered[3].astype(jnp.float32)
    bias_out = gathered[4].astype(jnp.float32)
    bias_fc2 = gathered[5].astype(jnp.float32)
    matrices = (gathered[6], gathered[7], gathered[8], gathered[9], gathered[10], gathered[11])
    qkv_weight = matrices[0]
    bias_qv = matrices[1].reshape(2, -1).astype(jnp.float32)
    out_weight = matrices[2]
    fc1_weight = matrices[3]
    bias_fc1 = matrices[4].reshape(-1).astype(jnp.float32)
    fc2_weight = matrices[5]
    micro_count, own_images, own_tokens, model_width = inputs.shape
    heads_local = qkv_weight.shape[2] // HD
    position = lax.axis_index("ctx") * own_tokens + jnp.arange(own_tokens)
    position_ok = position < SEQ_LEN
    acc_qkv = jnp.zeros(qkv_weight.shape, jnp.float32)
    acc_bias_qv = jnp.zeros((2, heads_local * HD), jnp.float32)
    acc_out = jnp.zeros(out_weight.shape, jnp.float32)
    acc_fc1 = jnp.zeros(fc1_weight.shape, jnp.float32)
    acc_bias_fc1 = jnp.zeros(bias_fc1.shape, jnp.float32)
    acc_fc2 = jnp.zeros(fc2_weight.shape, jnp.float32)
    vector_sums = [jnp.zeros((model_width,), jnp.float32) for column in range(6)]
    output_list = []
    input_list = []
    for micro_step in range(micro_count):
        rows_in = inputs[micro_step].astype(jnp.float32)
        valid_rows = ((slot_mask[micro_step] > 0)[:, None] & position_ok[None, :]).astype(
            jnp.float32
        )[:, :, None]
        normed_one, inv_one, scaled_one = normalize_rows(rows_in, gain_one, shift_one)
        group_rows = lax.all_gather(scaled_one.astype(jnp.bfloat16), "tp", axis=0, tiled=True)
        valid_keys = key_mask[micro_step] > 0
        group_size = group_rows.shape[0]
        joint_proj = jnp.einsum(
            "gcd,dke->gcke", group_rows, qkv_weight, preferred_element_type=jnp.float32
        )
        query_own = (joint_proj[:, :, 0] + bias_qv[0]).astype(jnp.bfloat16)
        key_own = joint_proj[:, :, 1].astype(jnp.bfloat16)
        value_own = (joint_proj[:, :, 2] + bias_qv[1]).astype(jnp.bfloat16)
        key_all, value_all = (
            lax.all_gather(key_own, "ctx", axis=1, tiled=True),
            lax.all_gather(value_own, "ctx", axis=1, tiled=True),
        )
        query_heads = query_own.reshape(group_size, own_tokens, heads_local, HD)
        key_heads = key_all.reshape(group_size, -1, heads_local, HD)
        value_heads = value_all.reshape(group_size, -1, heads_local, HD)
        scores = masked_scores(query_heads, key_heads, valid_keys)
        row_max = jnp.max(scores, axis=-1, keepdims=True)
        lifted = jnp.exp(scores - row_max)
        row_sum = jnp.sum(lifted, axis=-1, keepdims=True)
        log_total = row_max + jnp.log(row_sum)
        attention = (lifted / row_sum).astype(jnp.bfloat16)
        mixed_heads = jnp.einsum(
            "ghqk,gkhd->gqhd", attention, value_heads, preferred_element_type=jnp.float32
        )
        mixed_heads = mixed_heads.reshape(group_size, own_tokens, -1).astype(jnp.bfloat16)
        attn_out = lax.psum_scatter(
            row_product(mixed_heads, out_weight, "gce,ed->gcd").astype(jnp.bfloat16),
            "tp",
            scatter_dimension=0,
            tiled=True,
        ).astype(jnp.float32)
        hidden_one = rows_in + attn_out + bias_out
        normed_two, inv_two, scaled_two = normalize_rows(hidden_one, gain_two, shift_two)
        group_two = lax.all_gather(scaled_two.astype(jnp.bfloat16), "tp", axis=0, tiled=True)
        before = (
            jnp.einsum("gcd,df->gcf", group_two, fc1_weight, preferred_element_type=jnp.float32)
            + bias_fc1
        )
        gate_sig = jax.nn.sigmoid(1.702 * before)
        active = (before * gate_sig).astype(jnp.bfloat16)
        mlp_out = lax.psum_scatter(
            row_product(active, fc2_weight, "gcf,fd->gcd").astype(jnp.bfloat16),
            "tp",
            scatter_dimension=0,
            tiled=True,
        ).astype(jnp.float32)
        output_list.append(((hidden_one + mlp_out + bias_fc2) * valid_rows).astype(jnp.bfloat16))
        again = (
            lax.all_gather(ln1_gain, "fsdp", axis=0, tiled=True),
            lax.all_gather(ln2_gain, "fsdp", axis=0, tiled=True),
            lax.all_gather(w_qkv, "fsdp", axis=0, tiled=True),
            lax.all_gather(w_out, "fsdp", axis=1, tiled=True),
            lax.all_gather(w_fc1, "fsdp", axis=0, tiled=True),
            lax.all_gather(w_fc2, "fsdp", axis=1, tiled=True),
        )
        back_gain_one = again[0].astype(jnp.float32)
        back_gain_two = again[1].astype(jnp.float32)
        back_mats = (again[2], again[3], again[4], again[5])
        back_qkv = back_mats[0]
        back_out = back_mats[1]
        back_fc1 = back_mats[2]
        back_fc2 = back_mats[3]
        grad_out = cotangent[micro_step].astype(jnp.float32) * valid_rows
        vector_sums[5] = vector_sums[5] + jnp.sum(grad_out, axis=(0, 1))
        group_grad = lax.all_gather(grad_out.astype(jnp.bfloat16), "tp", axis=0, tiled=True)
        acc_fc2 = acc_fc2 + jnp.einsum(
            "gcf,gcd->fd", active, group_grad, preferred_element_type=jnp.float32
        )
        grad_active = jnp.einsum(
            "gcd,fd->gcf", group_grad, back_fc2, preferred_element_type=jnp.float32
        )
        grad_before = (
            grad_active * (gate_sig + 1.702 * before * gate_sig * (1.0 - gate_sig))
        ).astype(jnp.bfloat16)
        acc_bias_fc1 = acc_bias_fc1 + jnp.sum(grad_before, axis=(0, 1), dtype=jnp.float32)
        acc_fc1 = acc_fc1 + jnp.einsum(
            "gcd,gcf->df", group_two, grad_before, preferred_element_type=jnp.float32
        )
        grad_two = lax.psum_scatter(
            row_product(grad_before, back_fc1, "gcf,df->gcd").astype(jnp.bfloat16),
            "tp",
            scatter_dimension=0,
            tiled=True,
        ).astype(jnp.float32)
        vector_sums[2] = vector_sums[2] + jnp.sum(grad_two * normed_two, axis=(0, 1))
        vector_sums[3] = vector_sums[3] + jnp.sum(grad_two, axis=(0, 1))
        grad_hidden = grad_out + normalize_back(grad_two, normed_two, inv_two, back_gain_two)
        vector_sums[4] = vector_sums[4] + jnp.sum(grad_hidden, axis=(0, 1))
        group_hidden = lax.all_gather(grad_hidden.astype(jnp.bfloat16), "tp", axis=0, tiled=True)
        acc_out = acc_out + jnp.einsum(
            "gce,gcd->ed", mixed_heads, group_hidden, preferred_element_type=jnp.float32
        )
        grad_mixed = jnp.einsum(
            "gcd,ed->gce", group_hidden, back_out, preferred_element_type=jnp.float32
        ).astype(jnp.bfloat16)
        grad_mixed = grad_mixed.reshape(group_size, own_tokens, heads_local, HD)
        scores_again = masked_scores(query_heads, key_heads, valid_keys)
        soft_again = jnp.exp(scores_again - log_total)
        grad_soft = jnp.einsum(
            "gqhd,gkhd->ghqk", grad_mixed, value_heads, preferred_element_type=jnp.float32
        )
        inner_sum = jnp.sum(grad_soft * soft_again, axis=-1, keepdims=True)
        grad_scores = (soft_again * (grad_soft - inner_sum)).astype(jnp.bfloat16)
        grad_query = (
            jnp.einsum(
                "ghqk,gkhd->gqhd", grad_scores, key_heads, preferred_element_type=jnp.float32
            )
            * 0.125
        ).astype(jnp.bfloat16)
        key_part = (
            jnp.einsum(
                "ghqk,gqhd->gkhd", grad_scores, query_heads, preferred_element_type=jnp.float32
            )
            * 0.125
        )
        value_part = jnp.einsum(
            "ghqk,gqhd->gkhd",
            soft_again.astype(jnp.bfloat16),
            grad_mixed,
            preferred_element_type=jnp.float32,
        )
        key_grad, value_grad = (
            lax.psum_scatter(
                key_part.reshape(group_size, -1, heads_local * HD).astype(jnp.bfloat16),
                "ctx",
                scatter_dimension=1,
                tiled=True,
            ).astype(jnp.float32),
            lax.psum_scatter(
                value_part.reshape(group_size, -1, heads_local * HD).astype(jnp.bfloat16),
                "ctx",
                scatter_dimension=1,
                tiled=True,
            ).astype(jnp.float32),
        )
        grad_joint = jnp.stack(
            [
                grad_query.reshape(group_size, own_tokens, -1),
                key_grad.astype(jnp.bfloat16),
                value_grad.astype(jnp.bfloat16),
            ],
            axis=2,
        )
        acc_bias_qv = acc_bias_qv + jnp.stack(
            [
                jnp.sum(grad_joint[:, :, 0], axis=(0, 1), dtype=jnp.float32),
                jnp.sum(grad_joint[:, :, 2], axis=(0, 1), dtype=jnp.float32),
            ]
        )
        acc_qkv = acc_qkv + jnp.einsum(
            "gcd,gcke->dke", group_rows, grad_joint, preferred_element_type=jnp.float32
        )
        grad_one = lax.psum_scatter(
            row_product(grad_joint, back_qkv, "gcke,dke->gcd").astype(jnp.bfloat16),
            "tp",
            scatter_dimension=0,
            tiled=True,
        ).astype(jnp.float32)
        vector_sums[0] = vector_sums[0] + jnp.sum(grad_one * normed_one, axis=(0, 1))
        vector_sums[1] = vector_sums[1] + jnp.sum(grad_one, axis=(0, 1))
        input_list.append(
            (grad_hidden + normalize_back(grad_one, normed_one, inv_one, back_gain_one)).astype(
                jnp.bfloat16
            )
        )
    grad_parts = (
        acc_qkv,
        acc_bias_qv.reshape(2, heads_local, HD),
        acc_out,
        acc_fc1,
        acc_bias_fc1.reshape(-1, 64),
        acc_fc2,
    )
    matrix_sums = (
        lax.psum_scatter(
            grad_parts[0].astype(jnp.bfloat16), ("fsdp", "ctx"), scatter_dimension=0, tiled=True
        ).astype(jnp.float32),
        lax.psum_scatter(
            grad_parts[1].astype(jnp.bfloat16), ("fsdp", "ctx"), scatter_dimension=2, tiled=True
        ).astype(jnp.float32),
        lax.psum_scatter(
            grad_parts[2].astype(jnp.bfloat16), ("fsdp", "ctx"), scatter_dimension=1, tiled=True
        ).astype(jnp.float32),
        lax.psum_scatter(
            grad_parts[3].astype(jnp.bfloat16), ("fsdp", "ctx"), scatter_dimension=0, tiled=True
        ).astype(jnp.float32),
        lax.psum_scatter(
            grad_parts[4].astype(jnp.bfloat16), ("fsdp", "ctx"), scatter_dimension=1, tiled=True
        ).astype(jnp.float32),
        lax.psum_scatter(
            grad_parts[5].astype(jnp.bfloat16), ("fsdp", "ctx"), scatter_dimension=1, tiled=True
        ).astype(jnp.float32),
    )
    vector_part = lax.psum_scatter(
        jnp.stack(vector_sums), ("fsdp", "ctx", "tp"), scatter_dimension=1, tiled=True
    )
    return (
        jnp.stack(output_list),
        jnp.stack(input_list),
        vector_part[0],
        vector_part[1],
        matrix_sums[0],
        matrix_sums[1],
        matrix_sums[2],
        vector_part[4],
        vector_part[2],
        vector_part[3],
        matrix_sums[3],
        matrix_sums[4],
        matrix_sums[5],
        vector_part[5],
    )


def solution(mesh):
    in_specs = (
        P(None, ("fsdp", "tp"), "ctx", None),
        P(None, ("fsdp", "tp"), "ctx", None),
        P(None, ("fsdp", "tp")),
        P(None, "fsdp", None),
        P("fsdp"),
        P("fsdp"),
        P("fsdp", None, "tp"),
        P(None, "tp", "fsdp"),
        P("tp", "fsdp"),
        P("fsdp"),
        P("fsdp"),
        P("fsdp"),
        P("fsdp", "tp"),
        P("tp", "fsdp"),
        P("tp", "fsdp"),
        P("fsdp"),
    )
    out_specs = (
        P(None, ("fsdp", "tp"), "ctx", None),
        P(None, ("fsdp", "tp"), "ctx", None),
        P(("fsdp", "ctx", "tp")),
        P(("fsdp", "ctx", "tp")),
        P(("fsdp", "ctx"), None, "tp"),
        P(None, "tp", ("fsdp", "ctx")),
        P("tp", ("fsdp", "ctx")),
        P(("fsdp", "ctx", "tp")),
        P(("fsdp", "ctx", "tp")),
        P(("fsdp", "ctx", "tp")),
        P(("fsdp", "ctx"), "tp"),
        P("tp", ("fsdp", "ctx")),
        P("tp", ("fsdp", "ctx")),
        P(("fsdp", "ctx", "tp")),
    )
    return jax.shard_map(body, mesh=mesh, in_specs=in_specs, out_specs=out_specs, check_vma=False)
```

profile of v0, /device:TPU:0, one launch (start us, length us, event | category | flops | bytes accessed | tf_op | source)
XLA Modules:
  0.0 1203.3 jit_solution(1417948135517288823)
XLA Ops:
  7.2 22.5 %all-gather.2 = bf16[8,1,128]{2,1,0:T(2,128)(2,1)S(1)} all-gather(bf16[1,1,128]{2,1,0:T(2,128)(2,1)} %bitcast.462), channel_id=1, replica_groups=mesh['fsdp'=8,'ctx'=2,'tp'=2] {'fsdp'}, dimensions={0}, use_global_device_ids=true | all-gather | bytes 2304 | tf_op jit(solution)/shard_map/all_gather | solution.py:59
  29.7 16.4 %all-gather.3 = bf16[8,1,128]{2,1,0:T(2,128)(2,1)S(1)} all-gather(bf16[1,1,128]{2,1,0:T(2,128)(2,1)} %bitcast.463), channel_id=1, replica_groups=mesh['fsdp'=8,'ctx'=2,'tp'=2] {'fsdp'}, dimensions={0}, use_global_device_ids=true | all-gather | bytes 2304 | tf_op jit(solution)/shard_map/all_gather | solution.py:60
  51.8 6.5 all-gather.39.cloned.1.call-done
  58.3 63.9 %all-gather.27.cloned.1.call-done = bf16[1024,3,512]{2,0,1:T(8,128)(2,1)} async-done(((bf16[128,3,512]{2,0,1:T(8,128)(2,1)}), bf16[1024,3,512]{2,0,1:T(8,128)(2,1)}) %all-gather.27.cloned.1.call-update) | async-done | bytes 3145744 | tf_op jit(solution)/shard_map/all_gather | solution.py:65
  122.2 4.3 fusion.37
  129.4 30.4 %all_gather.88 = bf16[2,8,64]{1,0,2:T(2,128)(2,1)S(1)} all-gather(bf16[2,8,8]{1,0,2:T(2,128)(2,1)S(1)} %copy.164), channel_id=1, replica_groups=mesh['fsdp'=8,'ctx'=2,'tp'=2] {'fsdp'}, dimensions={2}, use_global_device_ids=true | all-gather | bytes 2304 | tf_op jit(solution)/shard_map/all_gather | solution.py:66
  160.0 4.3 fusion.39
  164.3 3.5 fusion.125
  177.1 2.6 copy.175
  179.7 3.8 fusion.16
  183.5 4.4 copy-done
  187.9 3.2 fusion.1
  192.8 6.7 fusion.92
  199.5 31.7 %all-gather.31.cloned.1.call-done = bf16[512,1024]{1,0:T(8,128)(2,1)} async-done(((bf16[512,128]{1,0:T(8,128)(2,1)}), bf16[512,1024]{1,0:T(8,128)(2,1)}) %all-gather.31.cloned.1.call-update) | async-done | bytes 1048592 | tf_op jit(solution)/shard_map/all_gather | solution.py:67
  231.2 3.1 convolution_convert_fusion
  234.9 19.9 %all-gather.53.cloned.1.call-done = bf16[2,592,1,512]{3,1,2,0:T(8,128)(2,1)} async-done(((bf16[2,296,1,512]{3,1,2,0:T(8,128)(2,1)}), bf16[2,592,1,512]{3,1,2,0:T(8,128)(2,1)}) %all-gather.53.cloned.1.call-update) | async-done | bytes 1212432 | tf_op jit(solution)/shard_map/all_gather | solution.py:114
  257.2 3.8 fusion.15
  261.0 4.6 copy-done.1
  265.7 3.2 fusion
  268.9 10.7 all-gather.29.cloned.1.call-done
  281.3 6.7 fusion.93
  291.6 20.4 %all-gather.4 = bf16[8,1,128]{2,1,0:T(2,128)(2,1)S(1)} all-gather(bf16[1,1,128]{2,1,0:T(2,128)(2,1)S(1)} %bitcast.464), channel_id=1, replica_groups=mesh['fsdp'=8,'ctx'=2,'tp'=2] {'fsdp'}, dimensions={0}, use_global_device_ids=true | all-gather | bytes 2304 | tf_op jit(solution)/shard_map/all_gather | solution.py:63
  312.0 16.4 %all-gather.5 = bf16[8,1,128]{2,1,0:T(2,128)(2,1)S(1)} all-gather(bf16[1,1,128]{2,1,0:T(2,128)(2,1)S(1)} %bitcast.465), channel_id=1, replica_groups=mesh['fsdp'=8,'ctx'=2,'tp'=2] {'fsdp'}, dimensions={0}, use_global_device_ids=true | all-gather | bytes 2304 | tf_op jit(solution)/shard_map/all_gather | solution.py:61
  328.4 18.3 %all-gather.6 = bf16[8,1,128]{2,1,0:T(2,128)(2,1)S(1)} all-gather(bf16[1,1,128]{2,1,0:T(2,128)(2,1)S(1)} %bitcast.466), channel_id=1, replica_groups=mesh['fsdp'=8,'ctx'=2,'tp'=2] {'fsdp'}, dimensions={0}, use_global_device_ids=true | all-gather | bytes 2304 | tf_op jit(solution)/shard_map/all_gather | solution.py:62
  352.9 2.6 fusion.129
  357.3 26.5 %all_gather.97 = bf16[32,64]{0,1:T(8,128)(2,1)S(1)} all-gather(bf16[32,8]{0,1:T(8,128)(2,1)S(1)} %copy-done.45), channel_id=1, replica_groups=mesh['fsdp'=8,'ctx'=2,'tp'=2] {'fsdp'}, dimensions={1}, use_global_device_ids=true | all-gather | bytes 4608 | tf_op jit(solution)/shard_map/all_gather | solution.py:69
  384.0 6.4 all-gather.43.cloned.1.call-done
  390.4 7.4 fusion.29
  397.8 4.6 all-gather.49.cloned.1.call-done
  402.4 78.1 %all-gather.37.cloned.1.call-done = bf16[2048,1024]{1,0:T(8,128)(2,1)} async-done(((bf16[2048,128]{1,0:T(8,128)(2,1)}), bf16[2048,1024]{1,0:T(8,128)(2,1)}) %all-gather.37.cloned.1.call-update) | async-done | bytes 4194320 | tf_op jit(solution)/shard_map/all_gather | solution.py:70
  480.5 8.8 convert_reduce_fusion
  490.7 3.8 fusion.67
  494.8 7.4 fusion.31
  502.2 8.8 convert_reduce_fusion.1
  512.4 3.8 fusion.64
  516.2 7.4 fusion.70
  524.0 7.7 fusion.73
  531.8 20.4 %all-gather.7 = bf16[8,1,128]{2,1,0:T(2,128)(2,1)S(1)} all-gather(bf16[1,1,128]{2,1,0:T(2,128)(2,1)S(1)} %bitcast.467), channel_id=1, replica_groups=mesh['fsdp'=8,'ctx'=2,'tp'=2] {'fsdp'}, dimensions={0}, use_global_device_ids=true | all-gather | bytes 2304 | tf_op jit(solution)/shard_map/all_gather | solution.py:64
  552.2 2.8 fusion.120
  555.1 3.3 fusion.128
  560.4 3.0 fusion.163
  569.5 6.1 fusion.58
  579.2 7.2 multiply_reduce_fusion.1
  586.4 6.9 multiply_convert_fusion.1
  601.5 6.2 fusion.61
  611.0 7.5 multiply_reduce_fusion
  618.6 6.8 multiply_convert_fusion
  631.2 4.7 convert_reduce_fusion.7
  642.8 5.3 bitcast_convert_fusion.1
  648.5 4.8 convert_reduce_fusion.6
  656.6 21.4 %reduce-scatter.57.cloned.1.call-done = bf16[296,1024]{1,0:T(8,128)(2,1)} async-done(((bf16[592,1024]{1,0:T(8,128)(2,1)}), bf16[296,1024]{1,0:T(8,128)(2,1)}) %reduce-scatter.57.cloned.1.call-update) | async-done | bytes 606224
  680.4 5.3 bitcast_convert_fusion
  690.9 6.0 fusion.162
  696.9 8.7 fusion.4
  705.7 5.7 fusion.171
  711.5 5.3 fusion.5
  717.1 7.2 fusion.134
  728.1 7.7 fusion.6
  738.9 43.9 %reduce-scatter.47.cloned.1.call-done = bf16[512,64]{0,1:T(8,128)(2,1)} async-done(((bf16[512,1024]{0,1:T(8,128)(2,1)}), bf16[512,64]{0,1:T(8,128)(2,1)}) %reduce-scatter.47.cloned.1.call-update) | async-done | bytes 65552 | tf_op jit(solution)/shard_map/reduce_scatter | solution.py:285
  785.8 73.3 %all-reduce.2 = (bf16[2,8,64]{1,0,2:T(2,128)(2,1)S(1)}, bf16[32,64]{1,0:T(8,128)(2,1)S(1)}) all-reduce(bf16[2,8,64]{1,0,2:T(2,128)(2,1)S(1)} %copy.187, bf16[32,64]{1,0:T(8,128)(2,1)S(1)} %convert_element_type.559), channel_id=18, replica_groups=mesh['fsdp'=8,'ctx'=2,'tp'=2] {'fsdp','ctx'}, use_global_device_ids=true, to_apply=%region_52.53.clone | all-reduce | flops 3072 | bytes 12288
  860.5 18.9 %reduce-scatter.51.cloned.1.call-done = bf16[2048,64]{0,1:T(8,128)(2,1)} async-done(((bf16[2048,1024]{0,1:T(8,128)(2,1)}), bf16[2048,64]{0,1:T(8,128)(2,1)}) %reduce-scatter.51.cloned.1.call-update) | async-done | bytes 262160 | tf_op jit(solution)/shard_map/reduce_scatter | solution.py:294
  881.1 95.2 %reduce-scatter.49.cloned.1.call-done = bf16[64,2048]{1,0:T(8,128)(2,1)} async-done(((bf16[1024,2048]{1,0:T(8,128)(2,1)}), bf16[64,2048]{1,0:T(8,128)(2,1)}) %reduce-scatter.49.cloned.1.call-update) | async-done | bytes 262160 | tf_op jit(solution)/shard_map/reduce_scatter | solution.py:288
  981.6 130.7 %reduce-scatter.61.cloned.1.call-done = f32[32,6]{1,0:T(8,128)} async-done(((f32[1024,6]{1,0:T(8,128)}), f32[32,6]{1,0:T(8,128)}) %reduce-scatter.61.cloned.1.call-update) | async-done | bytes 784
  1116.8 77.8 %reduce-scatter.45.cloned.1.call-done = bf16[64,3,512]{2,0,1:T(8,128)(2,1)} async-done(((bf16[1024,3,512]{2,0,1:T(8,128)(2,1)}), bf16[64,3,512]{2,0,1:T(8,128)(2,1)}) %reduce-scatter.45.cloned.1.call-update) | async-done | bytes 196624 | tf_op jit(solution)/shard_map/reduce_scatter | solution.py:279
  (332 shorter events, 109.0 us)
Async XLA Ops:
  7.2 40.5 %copy-start.2 = (bf16[2,1,296,1024]{3,2,1,0:T(8,128)(2,1)S(1)}, bf16[2,1,296,1024]{3,2,1,0:T(8,128)(2,1)}, u32[]{:S(2)}) copy-start(bf16[2,1,296,1024]{3,2,1,0:T(8,128)(2,1)} %param.16) | copy-start | bytes 3637252
  7.2 51.1 %all-gather.39.cloned.1.call-start = ((), (), s32[]{:S(2)}) async-start(), calls=%async_computation.26 | async-start | bytes 1818624 | tf_op jit(solution)/shard_map/all_gather | solution.py:104
  29.7 20.5 %copy-start.31 = (f32[8,1,128]{2,1,0:T(1,128)}, f32[8,1,128]{2,1,0:T(1,128)S(1)}, u32[]{:S(2)}) copy-start(f32[8,1,128]{2,1,0:T(1,128)S(1)} %convert_element_type.566) | copy-start | bytes 12292
  50.3 71.9 %all-gather.27.cloned.1.call-start = ((), (), s32[]{:S(2)}) async-start(), calls=%async_computation.18 | async-start | bytes 3538944 | tf_op jit(solution)/shard_map/all_gather | solution.py:65
  51.0 109.0 %all-gather.25.cloned.1.call-start = ((), (), s32[]{:S(2)}) async-start(), calls=%async_computation.17 | async-start | bytes 1818624 | tf_op jit(solution)/shard_map/all_gather | solution.py:104
  51.7 125.4 %all-gather.55.cloned.1.call-start = ((), (), s32[]{:S(2)}) async-start(), calls=%async_computation.44 | async-start | bytes 1818624 | tf_op jit(solution)/shard_map/all_gather | solution.py:114
  129.2 61.9 %all-gather.41.cloned.1.call-start = ((), (), s32[]{:S(2)}) async-start(), calls=%async_computation.27 | async-start | bytes 1818624 | tf_op jit(solution)/shard_map/all_gather | solution.py:115
  167.9 63.4 %all-gather.31.cloned.1.call-start = ((), (), s32[]{:S(2)}) async-start(), calls=%async_computation.20 | async-start | bytes 1179648 | tf_op jit(solution)/shard_map/all_gather | solution.py:67
  168.5 86.4 %all-gather.53.cloned.1.call-start = ((), (), s32[]{:S(2)}) async-start(), calls=%async_computation.43 | async-start | bytes 1818624 | tf_op jit(solution)/shard_map/all_gather | solution.py:114
  170.7 108.8 %all-gather.29.cloned.1.call-start = ((), (), s32[]{:S(2)}) async-start(), calls=%async_computation.19 | async-start | bytes 1818624 | tf_op jit(solution)/shard_map/all_gather | solution.py:115
  176.7 6.8 copy-start.8
  176.8 169.9 %reduce-scatter.33.cloned.1.call-start = ((), (), s32[]{:S(2)}) async-start(), calls=%async_computation.28 | async-start | bytes 1818624 | tf_op jit(solution)/shard_map/reduce_scatter | solution.py:130
  192.8 6.7 copy-start.19
  199.5 34.8 %copy-start.60 = (bf16[2,8,64,296]{3,2,1,0:T(8,128)(2,1)}, bf16[2,8,64,296]{3,2,1,0:T(8,128)(2,1)S(1)}, u32[]{:S(2)}) copy-start(bf16[2,8,64,296]{3,2,1,0:T(8,128)(2,1)S(1)} %fusion.92) | copy-start | bytes 1818628
  234.3 22.9 %copy-start.10 = (f32[2,296,1,512]{1,3,0,2:T(8,128)S(1)}, f32[2,296,1,512]{1,3,0,2:T(8,128)}, u32[]{:S(2)}) copy-start(f32[2,296,1,512]{1,3,0,2:T(8,128)} %copy.167) | copy-start | bytes 3637252
  234.3 112.3 %reduce-scatter.29.cloned.1.call-start = ((), (), s32[]{:S(2)}) async-start(), calls=%async_computation.21 | async-start | bytes 1818624 | tf_op jit(solution)/shard_map/reduce_scatter | solution.py:130
  261.0 4.6 copy-start.1
  281.3 6.7 copy-start.21
  281.3 7.6 copy-start.57
  290.8 21.2 %copy-start.48 = (bf16[128]{0:T(256)(128)(2,1)S(1)}, bf16[128]{0:T(256)(128)(2,1)}, u32[]{:S(2)}) copy-start(bf16[128]{0:T(256)(128)(2,1)} %param.26) | copy-start | bytes 772
  290.8 37.6 %copy-start.49 = (bf16[128]{0:T(256)(128)(2,1)S(1)}, bf16[128]{0:T(256)(128)(2,1)}, u32[]{:S(2)}) copy-start(bf16[128]{0:T(256)(128)(2,1)} %param.27) | copy-start | bytes 772
  290.8 93.2 %all-gather.35.cloned.1.call-start = ((), (), s32[]{:S(2)}) async-start(), calls=%async_computation.23 | async-start | bytes 4718592 | tf_op jit(solution)/shard_map/all_gather | solution.py:68
  291.5 98.8 %all-gather.43.cloned.1.call-start = ((), (), s32[]{:S(2)}) async-start(), calls=%async_computation.29 | async-start | bytes 1818624 | tf_op jit(solution)/shard_map/all_gather | solution.py:138
  350.9 51.4 %all-gather.49.cloned.1.call-start = ((), (), s32[]{:S(2)}) async-start(), calls=%async_computation.35 | async-start | bytes 1818624 | tf_op jit(solution)/shard_map/all_gather | solution.py:169
  355.5 125.0 %all-gather.37.cloned.1.call-start = ((), (), s32[]{:S(2)}) async-start(), calls=%async_computation.24 | async-start | bytes 4718592 | tf_op jit(solution)/shard_map/all_gather | solution.py:70
  356.1 138.7 %all-gather.33.cloned.1.call-start = ((), (), s32[]{:S(2)}) async-start(), calls=%async_computation.22 | async-start | bytes 1818624 | tf_op jit(solution)/shard_map/all_gather | solution.py:138
  356.7 145.5 %all-gather.45.cloned.1.call-start = ((), (), s32[]{:S(2)}) async-start(), calls=%async_computation.31 | async-start | bytes 1818624 | tf_op jit(solution)/shard_map/all_gather | solution.py:169
  357.3 194.9 %reduce-scatter.41.cloned.1.call-start = ((), (), s32[]{:S(2)}) async-start(), calls=%async_computation.36 | async-start | bytes 1818624 | tf_op jit(solution)/shard_map/reduce_scatter | solution.py:183
  480.5 10.2 copy-start.51
  494.5 57.7 %reduce-scatter.37.cloned.1.call-start = ((), (), s32[]{:S(2)}) async-start(), calls=%async_computation.32 | async-start | bytes 1818624 | tf_op jit(solution)/shard_map/reduce_scatter | solution.py:183
  502.2 10.2 copy-start.52
  516.2 38.8 %reduce-scatter.31.cloned.1.call-start = ((), (), s32[]{:S(2)}) async-start(), calls=%async_computation.25 | async-start | bytes 1818624 | tf_op jit(solution)/shard_map/reduce_scatter | solution.py:145
  523.7 8.0 copy-start.50
  523.7 36.7 %reduce-scatter.35.cloned.1.call-start = ((), (), s32[]{:S(2)}) async-start(), calls=%async_computation.30 | async-start | bytes 1818624 | tf_op jit(solution)/shard_map/reduce_scatter | solution.py:145
  531.7 35.3 %all-gather.47.cloned.1.call-start = ((), (), s32[]{:S(2)}) async-start(), calls=%async_computation.33 | async-start | bytes 1818624 | tf_op jit(solution)/shard_map/all_gather | solution.py:193
  560.3 38.6 %all-gather.51.cloned.1.call-start = ((), (), s32[]{:S(2)}) async-start(), calls=%async_computation.37 | async-start | bytes 1818624 | tf_op jit(solution)/shard_map/all_gather | solution.py:193
  565.4 71.7 %reduce-scatter.55.cloned.1.call-start = ((), (), s32[]{:S(2)}) async-start(), calls=%async_computation.46 | async-start | bytes 1818624
  578.7 60.8 %reduce-scatter.53.cloned.1.call-start = ((), (), s32[]{:S(2)}) async-start(), calls=%async_computation.45 | async-start | bytes 1818624
  586.4 6.9 copy-start.11
  598.9 55.5 %reduce-scatter.59.cloned.1.call-start = ((), (), s32[]{:S(2)}) async-start(), calls=%async_computation.48 | async-start | bytes 1818624
  610.8 67.3 %reduce-scatter.57.cloned.1.call-start = ((), (), s32[]{:S(2)}) async-start(), calls=%async_computation.47 | async-start | bytes 1818624
  618.6 6.8 copy-start.9
  631.1 93.2 %reduce-scatter.39.cloned.1.call-start = ((), (), s32[]{:S(2)}) async-start(), calls=%async_computation.34 | async-start | bytes 1818624 | tf_op jit(solution)/shard_map/reduce_scatter | solution.py:257
  639.5 8.7 copy-start.29
  642.8 5.6 copy-start.12
  648.2 76.1 %reduce-scatter.43.cloned.1.call-start = ((), (), s32[]{:S(2)}) async-start(), calls=%async_computation.38 | async-start | bytes 1818624 | tf_op jit(solution)/shard_map/reduce_scatter | solution.py:257
  656.6 23.8 %copy-start.18 = (bf16[296,2,512]{2,1,0:T(2,128)(2,1)}, bf16[296,2,512]{2,1,0:T(2,128)(2,1)S(1)}, u32[]{:S(2)}) copy-start(bf16[296,2,512]{2,1,0:T(2,128)(2,1)S(1)} %reshape.1103) | copy-start | bytes 1818628
  680.4 5.4 copy-start.55
  685.7 97.0 %reduce-scatter.47.cloned.1.call-start = ((), (), s32[]{:S(2)}) async-start(), calls=%async_computation.40 | async-start | bytes 1114112 | tf_op jit(solution)/shard_map/reduce_scatter | solution.py:285
  690.4 6.5 copy-start.54
  690.4 188.9 %reduce-scatter.51.cloned.1.call-start = ((), (), s32[]{:S(2)}) async-start(), calls=%async_computation.42 | async-start | bytes 4456448 | tf_op jit(solution)/shard_map/reduce_scatter | solution.py:294
  705.7 5.8 copy-start.53
  705.7 270.6 %reduce-scatter.49.cloned.1.call-start = ((), (), s32[]{:S(2)}) async-start(), calls=%async_computation.41 | async-start | bytes 4456448 | tf_op jit(solution)/shard_map/reduce_scatter | solution.py:288
  705.7 5.7 copy-start.66
  716.8 395.5 %reduce-scatter.61.cloned.1.call-start = ((), (), s32[]{:S(2)}) async-start(), calls=%async_computation.49 | async-start | bytes 540672
  717.0 7.3 copy-start.3
  717.1 7.3 copy-start.32
  717.1 7.3 copy-start.34
  717.1 7.3 copy-start.36
  717.1 7.3 copy-start.38
  717.1 7.3 copy-start.40
  728.0 466.6 %reduce-scatter.45.cloned.1.call-start = ((), (), s32[]{:S(2)}) async-start(), calls=%async_computation.39 | async-start | bytes 3342336 | tf_op jit(solution)/shard_map/reduce_scatter | solution.py:279
  738.9 239.3 %copy-start.15 = (f32[1,296,1024]{2,1,0:T(8,128)S(1)}, f32[1,296,1024]{2,1,0:T(8,128)}, u32[]{:S(2)}) copy-start(f32[1,296,1024]{2,1,0:T(8,128)} %copy-done.14) | copy-start | bytes 3637252
  785.6 192.5 %copy-start.28 = (bf16[1,296,1024]{2,1,0:T(8,128)(2,1)S(1)}, bf16[1,296,1024]{2,1,0:T(8,128)(2,1)}, u32[]{:S(2)}) copy-start(bf16[1,296,1024]{2,1,0:T(8,128)(2,1)} %reduce-scatter.39.cloned.1.call-done) | copy-start | bytes 1818628
  (37 other events, 72.6 us)
Sparse Core Ops, SparseCore 0:
  50.4 7.8 all-gather.38
  60.5 61.6 all-gather.26
  124.3 7.8 all-gather.24
  133.6 24.2 all-gather.54
  168.0 21.7 all-gather.40
  191.7 39.5 all-gather.30
  232.8 22.0 all-gather.52
  256.4 23.1 all-gather.28
  282.4 8.6 reduce-scatter.32
  293.8 9.8 reduce-scatter.28
  305.9 74.7 all-gather.34
  382.6 7.6 all-gather.42
  391.9 10.4 all-gather.48
  404.3 76.1 all-gather.36
  482.4 7.4 all-gather.32
  491.3 10.4 all-gather.44
  504.5 9.8 reduce-scatter.40
  517.1 9.8 reduce-scatter.36
  529.3 9.8 reduce-scatter.30
  541.3 9.8 reduce-scatter.34
  560.4 6.4 all-gather.46
  568.5 10.4 all-gather.50
  581.8 23.2 reduce-scatter.54
  607.3 22.1 reduce-scatter.52
  631.7 22.0 reduce-scatter.58
  655.9 22.1 reduce-scatter.56
  680.8 8.6 reduce-scatter.38
  691.7 9.8 reduce-scatter.42
  703.9 78.7 reduce-scatter.46
  785.0 94.2 reduce-scatter.50
  881.7 94.5 reduce-scatter.48
  978.7 133.5 reduce-scatter.60
  1114.4 80.1 reduce-scatter.44
where the time goes:
time: 1210 us; the launch traced here: 1200 us
  waiting for transfers between devices  616 us (51%)
  blocking collectives  245 us (20%)
  matrix products  189 us (16%)
  local copies, waits for them, and re-layouts  71.7 us (6%)
  other arithmetic  60 us (5%)
  between operations  18 us (1%)
    unnamed x38, waiting for transfers between devices  157 us
    reduce_scatter x1, waiting for transfers between devices, body(): lax.psum_scatter(grad_parts[3].astype(jnp.bfloat16), ('fsdp', 'ctx'), sca...  95.2 us
    all_gather x1, waiting for transfers between devices, body(): lax.all_gather(w_fc2, 'fsdp', axis=1, tiled=True)  78.1 us
    reduce_scatter x1, waiting for transfers between devices, body(): lax.psum_scatter(grad_parts[0].astype(jnp.bfloat16), ('fsdp', 'ctx'), sca...  77.8 us
    unnamed x1, blocking collectives  73.3 us
    all_gather x1, waiting for transfers between devices, body(): lax.all_gather(w_qkv, 'fsdp', axis=0, tiled=True)  63.9 us
    unnamed x161, local copies, waits for them, and re-layouts  49.1 us
    reduce_scatter x1, waiting for transfers between devices, body(): lax.psum_scatter(grad_parts[2].astype(jnp.bfloat16), ('fsdp', 'ctx'), sca...  43.9 us
  transfers between devices with their start and end apart: 33, of which 15 were waited for; matrix products, arithmetic and copies ran while one was open for 24% of the time, Pallas kernels for 0%

commit v1 on v0

--- a/solution.py
+++ b/solution.py
@@ -5,6 +5,22 @@
 
 HD = 64
 SEQ_LEN = 577
+
+
+def gather_around(x, axis, dim):
+    ways, here, step = (lax.axis_size(axis), lax.axis_index(axis), x.shape[dim])
+    dims = [n * ways if d == dim else n for d, n in enumerate(x.shape)]
+    full = lax.dynamic_update_slice_in_dim(jnp.zeros(dims, x.dtype), x, here * step, axis=dim)
+    going_up = going_down = x
+    for far in range(1, ways // 2 + 1):
+        going_up = lax.ppermute(going_up, axis, [(d, (d + 1) % ways) for d in range(ways)])
+        full = lax.dynamic_update_slice_in_dim(full, going_up, (here - far) % ways * step, axis=dim)
+        if 2 * far < ways:
+            going_down = lax.ppermute(going_down, axis, [(d, (d - 1) % ways) for d in range(ways)])
+            full = lax.dynamic_update_slice_in_dim(
+                full, going_down, (here + far) % ways * step, axis=dim
+            )
+    return full
 
 
 def normalize_rows(values, gain_row, shift_row):
@@ -66,7 +82,7 @@
         lax.all_gather(b_qv, "fsdp", axis=2, tiled=True),
         lax.all_gather(w_out, "fsdp", axis=1, tiled=True),
         lax.all_gather(w_fc1, "fsdp", axis=0, tiled=True),
-        lax.all_gather(b_fc1, "fsdp", axis=1, tiled=True),
+        gather_around(b_fc1, "fsdp", 1),
         lax.all_gather(w_fc2, "fsdp", axis=1, tiled=True),
     )
     gain_one = gathered[0].astype(jnp.float32)

time: 1210 us -> 1210 us (level)
  blocking collectives: 245 us -> 218 us
  waiting for transfers between devices: 616 us -> 629 us
    all_gather x1 -> x0, blocking collectives: 26.5 us -> none  [body(): lax.all_gather(b_fc1, 'fsdp', axis=1, tiled=True)]
    unnamed x161 -> x162, local copies, waits for them, and re-layouts: 49.1 us -> 49.2 us
  transfers between devices with their start and end apart: 33 -> 40, of which waited for: 15 -> 20; matrix products, arithmetic and copies ran while one was open for 24% -> 25% of each run, Pallas kernels for 0% -> 0%
where the time goes in v1:
time: 1210 us; the launch traced here: 1200 us
  waiting for transfers between devices  629 us (52%)
  blocking collectives  218 us (18%)
  matrix products  189 us (16%)
  local copies, waits for them, and re-layouts  74.4 us (6%)
  other arithmetic  59.8 us (5%)
  between operations  18.2 us (2%)
  starting transfers between devices  15.9 us (1%)
    unnamed x38, waiting for transfers between devices  157 us
    reduce_scatter x1, waiting for transfers between devices, body(): lax.psum_scatter(grad_parts[3].astype(jnp.bfloat16), ('fsdp', 'ctx'), sca...  95.3 us
    all_gather x1, waiting for transfers between devices, body(): lax.all_gather(w_fc2, 'fsdp', axis=1, tiled=True)  78.1 us
    reduce_scatter x1, waiting for transfers between devices, body(): lax.psum_scatter(grad_parts[0].astype(jnp.bfloat16), ('fsdp', 'ctx'), sca...  77.8 us
    unnamed x1, blocking collectives  73.4 us
    all_gather x1, waiting for transfers between devices, body(): lax.all_gather(w_qkv, 'fsdp', axis=0, tiled=True)  63.9 us
    unnamed x162, local copies, waits for them, and re-layouts  49.2 us
    reduce_scatter x1, waiting for transfers between devices, body(): lax.psum_scatter(grad_parts[2].astype(jnp.bfloat16), ('fsdp', 'ctx'), sca...  43.8 us
  transfers between devices with their start and end apart: 40, of which 20 were waited for; matrix products, arithmetic and copies ran while one was open for 25% of the time, Pallas kernels for 0%

profile of v1, /device:TPU:0, one launch (start us, length us, event | category | flops | bytes accessed | tf_op | source)
XLA Modules:
  0.0 1203.6 jit_solution(14143195549475081126)
XLA Ops:
  7.2 22.5 %all-gather.2 = bf16[8,1,128]{2,1,0:T(2,128)(2,1)S(1)} all-gather(bf16[1,1,128]{2,1,0:T(2,128)(2,1)} %bitcast.462), channel_id=1, replica_groups=mesh['fsdp'=8,'ctx'=2,'tp'=2] {'fsdp'}, dimensions={0}, use_global_device_ids=true | all-gather | bytes 2304 | tf_op jit(solution)/shard_map/all_gather | solution.py:75
  29.7 16.4 %all-gather.3 = bf16[8,1,128]{2,1,0:T(2,128)(2,1)S(1)} all-gather(bf16[1,1,128]{2,1,0:T(2,128)(2,1)} %bitcast.463), channel_id=1, replica_groups=mesh['fsdp'=8,'ctx'=2,'tp'=2] {'fsdp'}, dimensions={0}, use_global_device_ids=true | all-gather | bytes 2304 | tf_op jit(solution)/shard_map/all_gather | solution.py:76
  51.8 6.5 all-gather.39.cloned.1.call-done
  58.3 63.9 %all-gather.27.cloned.1.call-done = bf16[1024,3,512]{2,0,1:T(8,128)(2,1)} async-done(((bf16[128,3,512]{2,0,1:T(8,128)(2,1)}), bf16[1024,3,512]{2,0,1:T(8,128)(2,1)}) %all-gather.27.cloned.1.call-update) | async-done | bytes 3145744 | tf_op jit(solution)/shard_map/all_gather | solution.py:81
  122.2 4.3 fusion.37
  129.4 30.4 %all_gather.85 = bf16[2,8,64]{1,0,2:T(2,128)(2,1)S(1)} all-gather(bf16[2,8,8]{1,0,2:T(2,128)(2,1)S(1)} %copy.122), channel_id=1, replica_groups=mesh['fsdp'=8,'ctx'=2,'tp'=2] {'fsdp'}, dimensions={2}, use_global_device_ids=true | all-gather | bytes 2304 | tf_op jit(solution)/shard_map/all_gather | solution.py:82
  160.0 4.3 fusion.39
  164.3 3.6 fusion.125
  179.7 3.8 fusion.16
  183.5 4.4 copy-done
  187.9 3.2 fusion.1
  192.9 6.7 fusion.92
  199.6 31.7 %all-gather.31.cloned.1.call-done = bf16[512,1024]{1,0:T(8,128)(2,1)} async-done(((bf16[512,128]{1,0:T(8,128)(2,1)}), bf16[512,1024]{1,0:T(8,128)(2,1)}) %all-gather.31.cloned.1.call-update) | async-done | bytes 1048592 | tf_op jit(solution)/shard_map/all_gather | solution.py:83
  231.3 3.1 convolution_convert_fusion
  234.9 19.9 %all-gather.53.cloned.1.call-done = bf16[2,592,1,512]{3,1,2,0:T(8,128)(2,1)} async-done(((bf16[2,296,1,512]{3,1,2,0:T(8,128)(2,1)}), bf16[2,592,1,512]{3,1,2,0:T(8,128)(2,1)}) %all-gather.53.cloned.1.call-update) | async-done | bytes 1212432 | tf_op jit(solution)/shard_map/all_gather | solution.py:130
  257.3 3.8 fusion.15
  261.1 4.6 copy-done.1
  265.7 3.2 fusion
  268.9 10.7 all-gather.29.cloned.1.call-done
  281.3 6.7 fusion.93
  291.6 20.4 %all-gather.4 = bf16[8,1,128]{2,1,0:T(2,128)(2,1)S(1)} all-gather(bf16[1,1,128]{2,1,0:T(2,128)(2,1)S(1)} %bitcast.464), channel_id=1, replica_groups=mesh['fsdp'=8,'ctx'=2,'tp'=2] {'fsdp'}, dimensions={0}, use_global_device_ids=true | all-gather | bytes 2304 | tf_op jit(solution)/shard_map/all_gather | solution.py:79
  312.0 16.4 %all-gather.5 = bf16[8,1,128]{2,1,0:T(2,128)(2,1)S(1)} all-gather(bf16[1,1,128]{2,1,0:T(2,128)(2,1)S(1)} %bitcast.465), channel_id=1, replica_groups=mesh['fsdp'=8,'ctx'=2,'tp'=2] {'fsdp'}, dimensions={0}, use_global_device_ids=true | all-gather | bytes 2304 | tf_op jit(solution)/shard_map/all_gather | solution.py:77
  328.4 18.3 %all-gather.6 = bf16[8,1,128]{2,1,0:T(2,128)(2,1)S(1)} all-gather(bf16[1,1,128]{2,1,0:T(2,128)(2,1)S(1)} %bitcast.466), channel_id=1, replica_groups=mesh['fsdp'=8,'ctx'=2,'tp'=2] {'fsdp'}, dimensions={0}, use_global_device_ids=true | all-gather | bytes 2304 | tf_op jit(solution)/shard_map/all_gather | solution.py:78
  359.0 4.2 collective-permute-done
  363.3 4.8 collective-permute-start.3
  370.2 4.9 collective-permute-start.5
  377.9 4.5 collective-permute-done.6
  382.9 7.5 all-gather.43.cloned.1.call-done
  390.4 7.4 fusion.29
  397.8 4.6 all-gather.49.cloned.1.call-done
  402.4 78.1 %all-gather.37.cloned.1.call-done = bf16[2048,1024]{1,0:T(8,128)(2,1)} async-done(((bf16[2048,128]{1,0:T(8,128)(2,1)}), bf16[2048,1024]{1,0:T(8,128)(2,1)}) %all-gather.37.cloned.1.call-update) | async-done | bytes 4194320 | tf_op jit(solution)/shard_map/all_gather | solution.py:86
  480.5 8.8 convert_reduce_fusion
  490.8 3.8 fusion.67
  494.8 7.4 fusion.31
  502.3 8.8 convert_reduce_fusion.1
  512.5 3.7 fusion.64
  516.3 7.4 fusion.70
  524.2 7.7 fusion.73
  532.0 20.3 %all-gather.7 = bf16[8,1,128]{2,1,0:T(2,128)(2,1)S(1)} all-gather(bf16[1,1,128]{2,1,0:T(2,128)(2,1)S(1)} %bitcast.467), channel_id=1, replica_groups=mesh['fsdp'=8,'ctx'=2,'tp'=2] {'fsdp'}, dimensions={0}, use_global_device_ids=true | all-gather | bytes 2304 | tf_op jit(solution)/shard_map/all_gather | solution.py:80
  555.1 3.3 fusion.128
  560.5 3.0 fusion.163
  569.5 6.1 fusion.58
  579.0 7.2 multiply_reduce_fusion.1
  586.2 6.7 multiply_convert_fusion.1
  601.1 6.2 fusion.61
  610.7 7.3 multiply_reduce_fusion
  618.0 6.8 multiply_convert_fusion
  630.6 4.7 convert_reduce_fusion.7
  642.2 5.3 bitcast_convert_fusion.1
  647.8 4.7 convert_reduce_fusion.6
  656.2 21.9 %reduce-scatter.57.cloned.1.call-done = bf16[296,1024]{1,0:T(8,128)(2,1)} async-done(((bf16[592,1024]{1,0:T(8,128)(2,1)}), bf16[296,1024]{1,0:T(8,128)(2,1)}) %reduce-scatter.57.cloned.1.call-update) | async-done | bytes 606224
  680.5 5.3 bitcast_convert_fusion
  691.0 6.0 fusion.162
  697.0 8.7 fusion.4
  705.9 5.7 fusion.171
  711.6 5.3 fusion.5
  717.3 7.2 fusion.134
  728.2 7.7 fusion.6
  739.0 43.8 %reduce-scatter.47.cloned.1.call-done = bf16[512,64]{0,1:T(8,128)(2,1)} async-done(((bf16[512,1024]{0,1:T(8,128)(2,1)}), bf16[512,64]{0,1:T(8,128)(2,1)}) %reduce-scatter.47.cloned.1.call-update) | async-done | bytes 65552 | tf_op jit(solution)/shard_map/reduce_scatter | solution.py:301
  785.9 73.4 %all-reduce.2 = (bf16[2,8,64]{1,0,2:T(2,128)(2,1)S(1)}, bf16[32,64]{1,0:T(8,128)(2,1)S(1)}) all-reduce(bf16[2,8,64]{1,0,2:T(2,128)(2,1)S(1)} %copy.152, bf16[32,64]{1,0:T(8,128)(2,1)S(1)} %convert_element_type.559), channel_id=18, replica_groups=mesh['fsdp'=8,'ctx'=2,'tp'=2] {'fsdp','ctx'}, use_global_device_ids=true, to_apply=%region_52.53.clone | all-reduce | flops 3072 | bytes 12288
  860.7 18.8 %reduce-scatter.51.cloned.1.call-done = bf16[2048,64]{0,1:T(8,128)(2,1)} async-done(((bf16[2048,1024]{0,1:T(8,128)(2,1)}), bf16[2048,64]{0,1:T(8,128)(2,1)}) %reduce-scatter.51.cloned.1.call-update) | async-done | bytes 262160 | tf_op jit(solution)/shard_map/reduce_scatter | solution.py:310
  881.2 95.3 %reduce-scatter.49.cloned.1.call-done = bf16[64,2048]{1,0:T(8,128)(2,1)} async-done(((bf16[1024,2048]{1,0:T(8,128)(2,1)}), bf16[64,2048]{1,0:T(8,128)(2,1)}) %reduce-scatter.49.cloned.1.call-update) | async-done | bytes 262160 | tf_op jit(solution)/shard_map/reduce_scatter | solution.py:304
  981.8 130.7 %reduce-scatter.61.cloned.1.call-done = f32[32,6]{1,0:T(8,128)} async-done(((f32[1024,6]{1,0:T(8,128)}), f32[32,6]{1,0:T(8,128)}) %reduce-scatter.61.cloned.1.call-update) | async-done | bytes 784
  1117.0 77.8 %reduce-scatter.45.cloned.1.call-done = bf16[64,3,512]{2,0,1:T(8,128)(2,1)} async-done(((bf16[1024,3,512]{2,0,1:T(8,128)(2,1)}), bf16[64,3,512]{2,0,1:T(8,128)(2,1)}) %reduce-scatter.45.cloned.1.call-update) | async-done | bytes 196624 | tf_op jit(solution)/shard_map/reduce_scatter | solution.py:295
  (361 shorter events, 124.0 us)
Async XLA Ops:
  7.2 40.5 %copy-start.2 = (bf16[2,1,296,1024]{3,2,1,0:T(8,128)(2,1)S(1)}, bf16[2,1,296,1024]{3,2,1,0:T(8,128)(2,1)}, u32[]{:S(2)}) copy-start(bf16[2,1,296,1024]{3,2,1,0:T(8,128)(2,1)} %param.16) | copy-start | bytes 3637252
  7.2 51.1 %all-gather.39.cloned.1.call-start = ((), (), s32[]{:S(2)}) async-start(), calls=%async_computation.26 | async-start | bytes 1818624 | tf_op jit(solution)/shard_map/all_gather | solution.py:120
  29.7 20.5 %copy-start.31 = (f32[8,1,128]{2,1,0:T(1,128)}, f32[8,1,128]{2,1,0:T(1,128)S(1)}, u32[]{:S(2)}) copy-start(f32[8,1,128]{2,1,0:T(1,128)S(1)} %convert_element_type.566) | copy-start | bytes 12292
  50.3 71.9 %all-gather.27.cloned.1.call-start = ((), (), s32[]{:S(2)}) async-start(), calls=%async_computation.18 | async-start | bytes 3538944 | tf_op jit(solution)/shard_map/all_gather | solution.py:81
  51.0 109.0 %all-gather.25.cloned.1.call-start = ((), (), s32[]{:S(2)}) async-start(), calls=%async_computation.17 | async-start | bytes 1818624 | tf_op jit(solution)/shard_map/all_gather | solution.py:120
  51.7 125.4 %all-gather.55.cloned.1.call-start = ((), (), s32[]{:S(2)}) async-start(), calls=%async_computation.44 | async-start | bytes 1818624 | tf_op jit(solution)/shard_map/all_gather | solution.py:130
  129.2 61.9 %all-gather.41.cloned.1.call-start = ((), (), s32[]{:S(2)}) async-start(), calls=%async_computation.27 | async-start | bytes 1818624 | tf_op jit(solution)/shard_map/all_gather | solution.py:131
  167.9 63.4 %all-gather.31.cloned.1.call-start = ((), (), s32[]{:S(2)}) async-start(), calls=%async_computation.20 | async-start | bytes 1179648 | tf_op jit(solution)/shard_map/all_gather | solution.py:83
  168.5 86.4 %all-gather.53.cloned.1.call-start = ((), (), s32[]{:S(2)}) async-start(), calls=%async_computation.43 | async-start | bytes 1818624 | tf_op jit(solution)/shard_map/all_gather | solution.py:130
  170.8 108.8 %all-gather.29.cloned.1.call-start = ((), (), s32[]{:S(2)}) async-start(), calls=%async_computation.19 | async-start | bytes 1818624 | tf_op jit(solution)/shard_map/all_gather | solution.py:131
  176.8 6.8 copy-start.8
  176.8 169.9 %reduce-scatter.33.cloned.1.call-start = ((), (), s32[]{:S(2)}) async-start(), calls=%async_computation.28 | async-start | bytes 1818624 | tf_op jit(solution)/shard_map/reduce_scatter | solution.py:146
  199.6 34.8 %copy-start.60 = (bf16[2,8,64,296]{3,2,1,0:T(8,128)(2,1)}, bf16[2,8,64,296]{3,2,1,0:T(8,128)(2,1)S(1)}, u32[]{:S(2)}) copy-start(bf16[2,8,64,296]{3,2,1,0:T(8,128)(2,1)S(1)} %fusion.92) | copy-start | bytes 1818628
  234.3 22.9 %copy-start.10 = (f32[2,296,1,512]{1,3,0,2:T(8,128)S(1)}, f32[2,296,1,512]{1,3,0,2:T(8,128)}, u32[]{:S(2)}) copy-start(f32[2,296,1,512]{1,3,0,2:T(8,128)} %copy.125) | copy-start | bytes 3637252
  234.4 112.3 %reduce-scatter.29.cloned.1.call-start = ((), (), s32[]{:S(2)}) async-start(), calls=%async_computation.21 | async-start | bytes 1818624 | tf_op jit(solution)/shard_map/reduce_scatter | solution.py:146
  281.3 6.7 copy-start.21
  281.3 7.6 copy-start.57
  290.8 21.2 %copy-start.48 = (bf16[128]{0:T(256)(128)(2,1)S(1)}, bf16[128]{0:T(256)(128)(2,1)}, u32[]{:S(2)}) copy-start(bf16[128]{0:T(256)(128)(2,1)} %param.26) | copy-start | bytes 772
  290.8 37.6 %copy-start.49 = (bf16[128]{0:T(256)(128)(2,1)S(1)}, bf16[128]{0:T(256)(128)(2,1)}, u32[]{:S(2)}) copy-start(bf16[128]{0:T(256)(128)(2,1)} %param.27) | copy-start | bytes 772
  290.8 92.1 %all-gather.35.cloned.1.call-start = ((), (), s32[]{:S(2)}) async-start(), calls=%async_computation.23 | async-start | bytes 4718592 | tf_op jit(solution)/shard_map/all_gather | solution.py:84
  291.5 98.9 %all-gather.43.cloned.1.call-start = ((), (), s32[]{:S(2)}) async-start(), calls=%async_computation.29 | async-start | bytes 1818624 | tf_op jit(solution)/shard_map/all_gather | solution.py:154
  351.0 51.5 %all-gather.49.cloned.1.call-start = ((), (), s32[]{:S(2)}) async-start(), calls=%async_computation.35 | async-start | bytes 1818624 | tf_op jit(solution)/shard_map/all_gather | solution.py:185
  355.5 125.0 %all-gather.37.cloned.1.call-start = ((), (), s32[]{:S(2)}) async-start(), calls=%async_computation.24 | async-start | bytes 4718592 | tf_op jit(solution)/shard_map/all_gather | solution.py:86
  356.1 138.7 %all-gather.33.cloned.1.call-start = ((), (), s32[]{:S(2)}) async-start(), calls=%async_computation.22 | async-start | bytes 1818624 | tf_op jit(solution)/shard_map/all_gather | solution.py:154
  356.7 145.6 %all-gather.45.cloned.1.call-start = ((), (), s32[]{:S(2)}) async-start(), calls=%async_computation.31 | async-start | bytes 1818624 | tf_op jit(solution)/shard_map/all_gather | solution.py:185
  356.7 6.6 collective-permute-start.1
  356.8 6.4 collective-permute-start
  358.8 193.4 %reduce-scatter.41.cloned.1.call-start = ((), (), s32[]{:S(2)}) async-start(), calls=%async_computation.36 | async-start | bytes 1818624 | tf_op jit(solution)/shard_map/reduce_scatter | solution.py:199
  363.3 6.5 collective-permute-start.2
  363.3 6.9 collective-permute-start.3
  369.7 6.3 collective-permute-start.4
  370.2 7.3 collective-permute-start.5
  376.0 6.4 collective-permute-start.6
  480.5 10.3 copy-start.51
  494.6 57.7 %reduce-scatter.37.cloned.1.call-start = ((), (), s32[]{:S(2)}) async-start(), calls=%async_computation.32 | async-start | bytes 1818624 | tf_op jit(solution)/shard_map/reduce_scatter | solution.py:199
  502.2 10.2 copy-start.52
  516.2 38.9 %reduce-scatter.31.cloned.1.call-start = ((), (), s32[]{:S(2)}) async-start(), calls=%async_computation.25 | async-start | bytes 1818624 | tf_op jit(solution)/shard_map/reduce_scatter | solution.py:161
  523.7 8.2 copy-start.50
  523.7 36.7 %reduce-scatter.35.cloned.1.call-start = ((), (), s32[]{:S(2)}) async-start(), calls=%async_computation.30 | async-start | bytes 1818624 | tf_op jit(solution)/shard_map/reduce_scatter | solution.py:161
  531.9 35.2 %all-gather.47.cloned.1.call-start = ((), (), s32[]{:S(2)}) async-start(), calls=%async_computation.33 | async-start | bytes 1818624 | tf_op jit(solution)/shard_map/all_gather | solution.py:209
  560.4 38.2 %all-gather.51.cloned.1.call-start = ((), (), s32[]{:S(2)}) async-start(), calls=%async_computation.37 | async-start | bytes 1818624 | tf_op jit(solution)/shard_map/all_gather | solution.py:209
  565.5 71.1 %reduce-scatter.55.cloned.1.call-start = ((), (), s32[]{:S(2)}) async-start(), calls=%async_computation.46 | async-start | bytes 1818624
  578.8 60.1 %reduce-scatter.53.cloned.1.call-start = ((), (), s32[]{:S(2)}) async-start(), calls=%async_computation.45 | async-start | bytes 1818624
  586.2 6.7 copy-start.11
  598.5 55.4 %reduce-scatter.59.cloned.1.call-start = ((), (), s32[]{:S(2)}) async-start(), calls=%async_computation.48 | async-start | bytes 1818624
  610.5 67.7 %reduce-scatter.57.cloned.1.call-start = ((), (), s32[]{:S(2)}) async-start(), calls=%async_computation.47 | async-start | bytes 1818624
  618.0 6.8 copy-start.9
  630.5 94.0 %reduce-scatter.39.cloned.1.call-start = ((), (), s32[]{:S(2)}) async-start(), calls=%async_computation.34 | async-start | bytes 1818624 | tf_op jit(solution)/shard_map/reduce_scatter | solution.py:273
  638.8 8.7 copy-start.29
  647.5 77.0 %reduce-scatter.43.cloned.1.call-start = ((), (), s32[]{:S(2)}) async-start(), calls=%async_computation.38 | async-start | bytes 1818624 | tf_op jit(solution)/shard_map/reduce_scatter | solution.py:273
  656.1 24.3 %copy-start.18 = (bf16[296,2,512]{2,1,0:T(2,128)(2,1)}, bf16[296,2,512]{2,1,0:T(2,128)(2,1)S(1)}, u32[]{:S(2)}) copy-start(bf16[296,2,512]{2,1,0:T(2,128)(2,1)S(1)} %reshape.1103) | copy-start | bytes 1818628
  685.8 97.0 %reduce-scatter.47.cloned.1.call-start = ((), (), s32[]{:S(2)}) async-start(), calls=%async_computation.40 | async-start | bytes 1114112 | tf_op jit(solution)/shard_map/reduce_scatter | solution.py:301
  690.5 188.9 %reduce-scatter.51.cloned.1.call-start = ((), (), s32[]{:S(2)}) async-start(), calls=%async_computation.42 | async-start | bytes 4456448 | tf_op jit(solution)/shard_map/reduce_scatter | solution.py:310
  705.8 270.7 %reduce-scatter.49.cloned.1.call-start = ((), (), s32[]{:S(2)}) async-start(), calls=%async_computation.41 | async-start | bytes 4456448 | tf_op jit(solution)/shard_map/reduce_scatter | solution.py:304
  716.9 395.5 %reduce-scatter.61.cloned.1.call-start = ((), (), s32[]{:S(2)}) async-start(), calls=%async_computation.49 | async-start | bytes 540672
  717.2 7.3 copy-start.3
  717.2 7.3 copy-start.32
  717.2 7.3 copy-start.34
  717.2 7.3 copy-start.36
  717.2 7.3 copy-start.38
  717.3 7.3 copy-start.40
  728.2 466.7 %reduce-scatter.45.cloned.1.call-start = ((), (), s32[]{:S(2)}) async-start(), calls=%async_computation.39 | async-start | bytes 3342336 | tf_op jit(solution)/shard_map/reduce_scatter | solution.py:295
  739.0 239.3 %copy-start.15 = (f32[1,296,1024]{2,1,0:T(8,128)S(1)}, f32[1,296,1024]{2,1,0:T(8,128)}, u32[]{:S(2)}) copy-start(f32[1,296,1024]{2,1,0:T(8,128)} %copy-done.14) | copy-start | bytes 3637252
  785.7 192.6 %copy-start.28 = (bf16[1,296,1024]{2,1,0:T(8,128)(2,1)S(1)}, bf16[1,296,1024]{2,1,0:T(8,128)(2,1)}, u32[]{:S(2)}) copy-start(bf16[1,296,1024]{2,1,0:T(8,128)(2,1)} %reduce-scatter.39.cloned.1.call-done) | copy-start | bytes 1818628
  (44 other events, 114.9 us)
Sparse Core Ops, SparseCore 0:
  50.4 7.8 all-gather.38
  60.5 61.6 all-gather.26
  124.3 7.8 all-gather.24
  133.6 24.2 all-gather.54
  168.0 21.7 all-gather.40
  191.7 39.5 all-gather.30
  232.8 22.0 all-gather.52
  256.4 23.1 all-gather.28
  282.4 8.6 reduce-scatter.32
  293.8 9.8 reduce-scatter.28
  305.9 74.9 all-gather.34
  382.8 7.5 all-gather.42
  391.9 10.4 all-gather.48
  404.3 76.1 all-gather.36
  482.5 7.4 all-gather.32
  491.4 10.4 all-gather.44
  504.5 9.8 reduce-scatter.40
  517.1 9.8 reduce-scatter.36
  529.3 9.8 reduce-scatter.30
  541.3 9.8 reduce-scatter.34
  560.5 6.5 all-gather.46
  568.6 10.4 all-gather.50
  581.9 23.2 reduce-scatter.54
  607.3 22.0 reduce-scatter.52
  631.7 22.1 reduce-scatter.58
  656.0 22.0 reduce-scatter.56
  680.8 8.7 reduce-scatter.38
  691.8 9.8 reduce-scatter.42
  704.0 78.7 reduce-scatter.46
  785.1 94.3 reduce-scatter.50
  881.9 94.5 reduce-scatter.48
  978.8 133.5 reduce-scatter.60
  1114.6 80.1 reduce-scatter.44
